TPU v7x, 128 devices: a whole 4x4x4 slice. The times are simulated.
128 devices in a mesh: dp: 8 (over x, core), feat: 16 (over z, y).
Axes of the slice: x: 4, y: 4, z: 4, core: 2. Of those that a mesh axis runs over, the one named last changes fastest.
Arguments:
- features: bfloat16 [12288, 65536], P('dp', 'feat'), may hold values from -64 to 64
- weight: float32 [16, 65536], P(None, 'feat'), may hold values from -1 to 1
- labels: int32 [12288], P('dp'), may hold values from 0 to 15
- sample_weight: int32 [12288], P('dp'), may hold values from 1 to 4
Outputs:
- logit_step: float32 [12288, 16], P('dp')
- mean_loss: float32 [], replicated
All inputs are finite; a program needn't handle non-finite values.
Results may differ from a plain program's by a relative error of at most 0.014.
Values may be sent and summed in bfloat16 or wider, within the bound.
A program may use at most 64 MiB of HBM per device.

v0:
```python
import jax
import jax.numpy as jnp
from jax import lax
from jax.sharding import PartitionSpec as P

CG_ITERS = 4
RIDGE_COEF = 0.1
NORM_GUARD = 1e-06


def row_products(features, matrix_b):
    return lax.dot_general(
        features, matrix_b, (((1,), (1,)), ((), ())), preferred_element_type=jnp.float32
    )


def column_products(rows_b, features):
    return lax.dot_general(
        rows_b, features, (((0,), (0,)), ((), ())), preferred_element_type=jnp.float32
    )


def on_device(features, weight, labels, sample_weight):
    classes = weight.shape[0]
    weight_b = weight.astype(jnp.bfloat16)
    logits = lax.psum(row_products(features, weight_b), "feat")
    row_top = jnp.max(logits, axis=1, keepdims=True)
    shifted = jnp.exp(logits - row_top)
    summed = jnp.sum(shifted, axis=1, keepdims=True)
    class_prob = shifted / summed
    log_total = row_top[:, 0] + jnp.log(summed[:, 0])
    row_weight = sample_weight.astype(jnp.float32)
    onehot = (labels[:, None] == jnp.arange(classes, dtype=jnp.int32)[None, :]).astype(jnp.float32)
    picked = jnp.sum(logits * onehot, axis=1)
    weight_total, loss_total = lax.psum(
        (jnp.sum(row_weight), jnp.sum(row_weight * (log_total - picked))), "dp"
    )
    mean_loss = loss_total / weight_total
    row_scale = (row_weight / weight_total)[:, None]
    resid_rows = (row_scale * (class_prob - onehot)).astype(jnp.bfloat16)
    grad_partial = column_products(resid_rows, features)

    def inner_total(value):
        return lax.psum(value, "feat")

    gradient = (
        lax.psum(grad_partial.astype(jnp.bfloat16), "dp").astype(jnp.float32) + RIDGE_COEF * weight
    )
    newton_step = jnp.zeros_like(gradient)
    residual = -gradient
    direction = residual
    res_norm = inner_total(jnp.sum(residual * residual))
    for _ in range(CG_ITERS):
        direction_b = direction.astype(jnp.bfloat16)
        dir_scores = lax.psum(
            row_products(features, direction_b).astype(jnp.bfloat16), "feat"
        ).astype(jnp.float32)
        mixed_mean = jnp.sum(class_prob * dir_scores, axis=1, keepdims=True)
        curv_rows = (row_scale * class_prob * (dir_scores - mixed_mean)).astype(jnp.bfloat16)
        hess_image = (
            lax.psum(column_products(curv_rows, features).astype(jnp.bfloat16), "dp").astype(
                jnp.float32
            )
            + RIDGE_COEF * direction
        )
        step_size = res_norm / inner_total(jnp.sum(direction * hess_image))
        newton_step = newton_step + step_size * direction
        residual = residual - step_size * hess_image
        new_norm = inner_total(jnp.sum(residual * residual))
        direction = residual + new_norm / (res_norm + NORM_GUARD) * direction
        res_norm = new_norm
    step_b = newton_step.astype(jnp.bfloat16)
    logit_step = lax.psum(row_products(features, step_b).astype(jnp.bfloat16), "feat").astype(
        jnp.float32
    )
    return (logit_step, mean_loss)


def solution(mesh):
    in_specs = (P("dp", "feat"), P(None, "feat"), P("dp"), P("dp"))
    out_specs = (P("dp", None), P())
    return jax.shard_map(
        on_device, mesh=mesh, in_specs=in_specs, out_specs=out_specs, check_vma=False
    )
```

profile of v0, /device:TPU:0, one launch (start us, length us, event | category | flops | bytes accessed | tf_op | source)
XLA Modules:
  0.0 1117.8 jit_solution(13051484265639094176)
XLA Ops:
  8.5 8.6 fusion.12
  17.2 15.4 %psum.147 = f32[]{:T(128)} all-reduce(f32[]{:T(128)} %convert_reduce_fusion), channel_id=1, replica_groups=mesh['dp'=8,'feat'=16] {'dp'}, use_global_device_ids=true, to_apply=%region_1.0 | all-reduce | flops 1 | bytes 8 | tf_op jit(solution)/shard_map/psum | solution.py:35
  33.2 69.7 %all-reduce.8.cloned.1.call-done = f32[1536,16]{0,1:T(8,128)} async-done(((f32[1536,16]{0,1:T(8,128)}), f32[1536,16]{0,1:T(8,128)}) %all-reduce.8.cloned.1.call-update) | async-done | bytes 98320 | tf_op jit(solution)/shard_map/psum | solution.py:26
  104.8 7.1 convolution_convert_fusion.4
  111.9 58.6 %all-reduce.10.cloned.1.call-done = bf16[16,4096]{1,0:T(8,128)(2,1)} async-done(((bf16[16,4096]{1,0:T(8,128)(2,1)}), bf16[16,4096]{1,0:T(8,128)(2,1)}) %all-reduce.10.cloned.1.call-update) | async-done | bytes 131088 | tf_op jit(solution)/shard_map/psum | solution.py:47
  171.5 7.9 fusion
  179.4 74.6 %psum.151 = bf16[1536,16]{0,1:T(8,128)(2,1)S(1)} all-reduce(bf16[1536,16]{0,1:T(8,128)(2,1)S(1)} %fusion), channel_id=1, replica_groups=mesh['dp'=8,'feat'=16] {'feat'}, use_global_device_ids=true, to_apply=%region_8.0 | all-reduce | flops 24576 | bytes 98304 | tf_op jit(solution)/shard_map/psum | solution.py:55
  254.1 7.0 convolution_convert_fusion.3
  261.1 53.6 %all-reduce.12.cloned.1.call-done = bf16[16,4096]{1,0:T(8,128)(2,1)} async-done(((bf16[16,4096]{1,0:T(8,128)(2,1)}), bf16[16,4096]{1,0:T(8,128)(2,1)}) %all-reduce.12.cloned.1.call-update) | async-done | bytes 131088 | tf_op jit(solution)/shard_map/psum | solution.py:61
  316.3 41.3 %all-reduce = (f32[]{:T(128)}, f32[]{:T(128)}) all-reduce(f32[]{:T(128)} %get-tuple-element.3, f32[]{:T(128)} %get-tuple-element.2), channel_id=1, replica_groups=mesh['dp'=8,'feat'=16] {'feat'}, use_global_device_ids=true, to_apply=%region_7.0 | all-reduce | flops 2 | bytes 16 | tf_op jit(solution)/shard_map/psum | solution.py:44
  361.2 36.3 %psum.154 = f32[]{:T(128)} all-reduce(f32[]{:T(128)} %multiply_reduce_fusion.5), channel_id=1, replica_groups=mesh['dp'=8,'feat'=16] {'feat'}, use_global_device_ids=true, to_apply=%region_14.0 | all-reduce | flops 1 | bytes 8 | tf_op jit(solution)/shard_map/psum | solution.py:44
  398.2 8.0 fusion.1
  406.2 71.7 %psum.155 = bf16[1536,16]{0,1:T(8,128)(2,1)S(1)} all-reduce(bf16[1536,16]{0,1:T(8,128)(2,1)S(1)} %fusion.1), channel_id=1, replica_groups=mesh['dp'=8,'feat'=16] {'feat'}, use_global_device_ids=true, to_apply=%region_15.0 | all-reduce | flops 24576 | bytes 98304 | tf_op jit(solution)/shard_map/psum | solution.py:55
  477.9 7.0 convolution_convert_fusion.2
  484.9 53.6 %all-reduce.14.cloned.1.call-done = bf16[16,4096]{1,0:T(8,128)(2,1)} async-done(((bf16[16,4096]{1,0:T(8,128)(2,1)}), bf16[16,4096]{1,0:T(8,128)(2,1)}) %all-reduce.14.cloned.1.call-update) | async-done | bytes 131088 | tf_op jit(solution)/shard_map/psum | solution.py:61
  540.2 41.3 %psum.157 = f32[]{:T(128)} all-reduce(f32[]{:T(128)} %multiply_reduce_fusion.4), channel_id=1, replica_groups=mesh['dp'=8,'feat'=16] {'feat'}, use_global_device_ids=true, to_apply=%region_19.0 | all-reduce | flops 1 | bytes 8 | tf_op jit(solution)/shard_map/psum | solution.py:44
  585.2 36.0 %psum.158 = f32[]{:T(128)} all-reduce(f32[]{:T(128)} %multiply_reduce_fusion.3), channel_id=1, replica_groups=mesh['dp'=8,'feat'=16] {'feat'}, use_global_device_ids=true, to_apply=%region_21.0 | all-reduce | flops 1 | bytes 8 | tf_op jit(solution)/shard_map/psum | solution.py:44
  621.9 8.0 fusion.2
  629.9 71.7 %psum.159 = bf16[1536,16]{0,1:T(8,128)(2,1)S(1)} all-reduce(bf16[1536,16]{0,1:T(8,128)(2,1)S(1)} %fusion.2), channel_id=1, replica_groups=mesh['dp'=8,'feat'=16] {'feat'}, use_global_device_ids=true, to_apply=%region_22.0 | all-reduce | flops 24576 | bytes 98304 | tf_op jit(solution)/shard_map/psum | solution.py:55
  701.6 7.0 convolution_convert_fusion.1
  708.6 53.6 %all-reduce.16.cloned.1.call-done = bf16[16,4096]{1,0:T(8,128)(2,1)} async-done(((bf16[16,4096]{1,0:T(8,128)(2,1)}), bf16[16,4096]{1,0:T(8,128)(2,1)}) %all-reduce.16.cloned.1.call-update) | async-done | bytes 131088 | tf_op jit(solution)/shard_map/psum | solution.py:61
  763.9 41.2 %psum.161 = f32[]{:T(128)} all-reduce(f32[]{:T(128)} %multiply_reduce_fusion.2), channel_id=1, replica_groups=mesh['dp'=8,'feat'=16] {'feat'}, use_global_device_ids=true, to_apply=%region_26.0 | all-reduce | flops 1 | bytes 8 | tf_op jit(solution)/shard_map/psum | solution.py:44
  808.7 36.2 %psum.162 = f32[]{:T(128)} all-reduce(f32[]{:T(128)} %multiply_reduce_fusion.1), channel_id=1, replica_groups=mesh['dp'=8,'feat'=16] {'feat'}, use_global_device_ids=true, to_apply=%region_28.0 | all-reduce | flops 1 | bytes 8 | tf_op jit(solution)/shard_map/psum | solution.py:44
  845.6 8.0 fusion.3
  853.6 71.7 %psum.163 = bf16[1536,16]{0,1:T(8,128)(2,1)S(1)} all-reduce(bf16[1536,16]{0,1:T(8,128)(2,1)S(1)} %fusion.3), channel_id=1, replica_groups=mesh['dp'=8,'feat'=16] {'feat'}, use_global_device_ids=true, to_apply=%region_29.0 | all-reduce | flops 24576 | bytes 98304 | tf_op jit(solution)/shard_map/psum | solution.py:55
  925.3 7.0 convolution_convert_fusion
  933.0 13.1 %psum.167 = f32[]{:T(128)} all-reduce(f32[]{:T(128)} %multiply_reduce_fusion.8), channel_id=1, replica_groups=mesh['dp'=8,'feat'=16] {'dp'}, use_global_device_ids=true, to_apply=%region_37.0 | all-reduce | flops 1 | bytes 8 | tf_op jit(solution)/shard_map/psum | solution.py:35
  946.1 39.8 %all-reduce.18.cloned.1.call-done = bf16[16,4096]{1,0:T(8,128)(2,1)} async-done(((bf16[16,4096]{1,0:T(8,128)(2,1)}), bf16[16,4096]{1,0:T(8,128)(2,1)}) %all-reduce.18.cloned.1.call-update) | async-done | bytes 131088 | tf_op jit(solution)/shard_map/psum | solution.py:61
  985.9 1.8 multiply_reduce_fusion
  989.1 41.2 %psum.165 = f32[]{:T(128)} all-reduce(f32[]{:T(128)} %multiply_reduce_fusion), channel_id=1, replica_groups=mesh['dp'=8,'feat'=16] {'feat'}, use_global_device_ids=true, to_apply=%region_33.0 | all-reduce | flops 1 | bytes 8 | tf_op jit(solution)/shard_map/psum | solution.py:44
  1031.6 7.9 fusion.4
  1039.5 69.6 %psum.166 = bf16[1536,16]{0,1:T(8,128)(2,1)S(1)} all-reduce(bf16[1536,16]{0,1:T(8,128)(2,1)S(1)} %fusion.4), channel_id=1, replica_groups=mesh['dp'=8,'feat'=16] {'feat'}, use_global_device_ids=true, to_apply=%region_34.0 | all-reduce | flops 24576 | bytes 98304 | tf_op jit(solution)/shard_map/psum | solution.py:73
  (43 shorter events, 16.6 us)
Async XLA Ops:
  7.2 25.4 %copy-start.5 = (s32[1536]{0:T(1024)S(1)}, s32[1536]{0:T(1024)}, u32[]{:S(2)}) copy-start(s32[1536]{0:T(1024)} %param.7) | copy-start | bytes 18436
  7.2 97.6 %copy-start.6 = (s32[1536]{0:T(1024)S(1)}, s32[1536]{0:T(1024)}, u32[]{:S(2)}) copy-start(s32[1536]{0:T(1024)} %param.6) | copy-start | bytes 18436
  7.2 95.7 %all-reduce.8.cloned.1.call-start = ((), (), s32[]{:S(2)}) async-start(), calls=%async_computation | async-start | bytes 196608 | tf_op jit(solution)/shard_map/psum | solution.py:26
  17.1 153.4 %copy-start.4 = (f32[16,4096]{1,0:T(8,128)S(1)}, f32[16,4096]{1,0:T(8,128)}, u32[]{:S(2)}) copy-start(f32[16,4096]{1,0:T(8,128)} %param.5) | copy-start | bytes 786436
  17.1 153.4 %all-reduce.10.cloned.1.call-start = ((), (), s32[]{:S(2)}) async-start(), calls=%async_computation.1 | async-start | bytes 262144 | tf_op jit(solution)/shard_map/psum | solution.py:47
  104.8 149.2 %copy-start = (f32[1536,16]{0,1:T(8,128)S(1)}, f32[1536,16]{0,1:T(8,128)}, u32[]{:S(2)}) copy-start(f32[1536,16]{0,1:T(8,128)} %all-reduce.8.cloned.1.call-done) | copy-start | bytes 294916
  111.9 202.9 %all-reduce.12.cloned.1.call-start = ((), (), s32[]{:S(2)}) async-start(), calls=%async_computation.2 | async-start | bytes 262144 | tf_op jit(solution)/shard_map/psum | solution.py:61
  261.1 277.4 %all-reduce.14.cloned.1.call-start = ((), (), s32[]{:S(2)}) async-start(), calls=%async_computation.3 | async-start | bytes 262144 | tf_op jit(solution)/shard_map/psum | solution.py:61
  406.2 132.3 %copy-start.1 = (bf16[16,4096]{1,0:T(8,128)(2,1)S(1)}, bf16[16,4096]{1,0:T(8,128)(2,1)}, u32[]{:S(2)}) copy-start(bf16[16,4096]{1,0:T(8,128)(2,1)} %all-reduce.12.cloned.1.call-done) | copy-start | bytes 393220
  484.9 277.4 %all-reduce.16.cloned.1.call-start = ((), (), s32[]{:S(2)}) async-start(), calls=%async_computation.4 | async-start | bytes 262144 | tf_op jit(solution)/shard_map/psum | solution.py:61
  629.9 132.4 %copy-start.2 = (bf16[16,4096]{1,0:T(8,128)(2,1)S(1)}, bf16[16,4096]{1,0:T(8,128)(2,1)}, u32[]{:S(2)}) copy-start(bf16[16,4096]{1,0:T(8,128)(2,1)} %all-reduce.14.cloned.1.call-done) | copy-start | bytes 393220
  708.6 277.3 %all-reduce.18.cloned.1.call-start = ((), (), s32[]{:S(2)}) async-start(), calls=%async_computation.5 | async-start | bytes 262144 | tf_op jit(solution)/shard_map/psum | solution.py:61
  853.6 132.3 %copy-start.3 = (bf16[16,4096]{1,0:T(8,128)(2,1)S(1)}, bf16[16,4096]{1,0:T(8,128)(2,1)}, u32[]{:S(2)}) copy-start(bf16[16,4096]{1,0:T(8,128)(2,1)} %all-reduce.16.cloned.1.call-done) | copy-start | bytes 393220
Sparse Core Ops, SparseCore 0:
  17.3 85.6 all-reduce.7
  112.0 58.4 all-reduce.9
  261.2 53.4 all-reduce.11
  485.0 53.4 all-reduce.13
  708.7 53.4 all-reduce.15
  932.4 53.4 all-reduce.17
where the time goes:
time: 1120 us
  blocking collectives  661 us (59%)
  waiting for transfers between devices  329 us (29%)
  matrix products  83.4 us (7%)
  between operations  26 us (2%)
  other arithmetic  18 us (2%)
    psum x4, blocking collectives, on_device(): lax.psum(row_products(features, direction_b).astype(jnp.bfloat16), 'feat')  290 us
    psum x7, blocking collectives, inner_total(): return lax.psum(value, 'feat')  273 us
    psum x4, waiting for transfers between devices, on_device(): lax.psum(column_products(curv_rows, features).astype(jnp.bfloat16), 'dp')  201 us
    psum x1, waiting for transfers between devices, on_device(): logits = lax.psum(row_products(features, weight_b), 'feat')  69.7 us
    psum x1, blocking collectives, on_device(): lax.psum(row_products(features, step_b).astype(jnp.bfloat16), 'feat')  69.6 us
    psum x1, waiting for transfers between devices, on_device(): lax.psum(grad_partial.astype(jnp.bfloat16), 'dp').astype(jnp.float32)  58.6 us
    dot_general x6, matrix products, row_products(): lax.dot_general(features, matrix_b, (((1,), (1,)), ((), ())), preferred_e...  48.4 us
    dot_general x5, matrix products, column_products(): lax.dot_general(rows_b, features, (((0,), (0,)), ((), ())), preferred_ele...  35 us
  transfers between devices with their start and end apart: 6, of which 6 were waited for; matrix products, arithmetic and copies ran while one was open for 0% of the time, Pallas kernels for 0%

commit v1 on v0

--- a/solution.py
+++ b/solution.py
@@ -23,7 +23,7 @@
 def on_device(features, weight, labels, sample_weight):
     classes = weight.shape[0]
     weight_b = weight.astype(jnp.bfloat16)
-    logits = lax.psum(row_products(features, weight_b), "feat")
+    logits = jnp.sum(lax.all_gather(row_products(features, weight_b), "feat"), axis=0)
     row_top = jnp.max(logits, axis=1, keepdims=True)
     shifted = jnp.exp(logits - row_top)
     summed = jnp.sum(shifted, axis=1, keepdims=True)

time: 1120 us -> 1080 us (0.964)
  waiting for transfers between devices: 329 us -> 290 us
    psum x1 -> x0, waiting for transfers between devices: 69.7 us -> none  [on_device(): logits = lax.psum(row_products(features, weight_b), 'feat')]
    all_gather x0 -> x1, waiting for transfers between devices: none -> 29.8 us  [on_device(): lax.all_gather(row_products(features, weight_b), 'feat')]
where the time goes in v1:
time: 1080 us
  blocking collectives  661 us (61%)
  waiting for transfers between devices  290 us (27%)
  matrix products  83.3 us (8%)
  between operations  26 us (2%)
  other arithmetic  15.8 us (1%)
    psum x4, blocking collectives, on_device(): lax.psum(row_products(features, direction_b).astype(jnp.bfloat16), 'feat')  290 us
    psum x7, blocking collectives, inner_total(): return lax.psum(value, 'feat')  273 us
    psum x4, waiting for transfers between devices, on_device(): lax.psum(column_products(curv_rows, features).astype(jnp.bfloat16), 'dp')  201 us
    psum x1, blocking collectives, on_device(): lax.psum(row_products(features, step_b).astype(jnp.bfloat16), 'feat')  69.6 us
    psum x1, waiting for transfers between devices, on_device(): lax.psum(grad_partial.astype(jnp.bfloat16), 'dp').astype(jnp.float32)  59.2 us
    dot_general x6, matrix products, row_products(): lax.dot_general(features, matrix_b, (((1,), (1,)), ((), ())), preferred_e...  48.4 us
    dot_general x5, matrix products, column_products(): lax.dot_general(rows_b, features, (((0,), (0,)), ((), ())), preferred_ele...  34.9 us
    all_gather x1, waiting for transfers between devices, on_device(): lax.all_gather(row_products(features, weight_b), 'feat')  29.8 us
  transfers between devices with their start and end apart: 6, of which 6 were waited for; matrix products, arithmetic and copies ran while one was open for 0% of the time, Pallas kernels for 0%

profile of v1, /device:TPU:0, one launch (start us, length us, event | category | flops | bytes accessed | tf_op | source)
XLA Modules:
  0.0 1078.5 jit_solution(10470772019572565474)
XLA Ops:
  7.2 8.6 fusion.12
  16.5 15.3 %psum.140 = f32[]{:T(128)} all-reduce(f32[]{:T(128)} %convert_reduce_fusion), channel_id=1, replica_groups=mesh['dp'=8,'feat'=16] {'dp'}, use_global_device_ids=true, to_apply=%region_1.0 | all-reduce | flops 1 | bytes 8 | tf_op jit(solution)/shard_map/psum | solution.py:35
  32.5 29.8 %all-gather.3.cloned.1.call-done = f32[24576,16]{0,1:T(8,128)} async-done(((f32[1536,16]{0,1:T(8,128)}), f32[24576,16]{0,1:T(8,128)}) %all-gather.3.cloned.1.call-update) | async-done | bytes 1572880 | tf_op jit(solution)/shard_map/all_gather | solution.py:26
  62.3 2.3 copy.6
  65.0 7.0 convolution_convert_fusion.4
  72.0 59.2 %all-reduce.7.cloned.1.call-done = bf16[16,4096]{1,0:T(8,128)(2,1)} async-done(((bf16[16,4096]{1,0:T(8,128)(2,1)}), bf16[16,4096]{1,0:T(8,128)(2,1)}) %all-reduce.7.cloned.1.call-update) | async-done | bytes 131088 | tf_op jit(solution)/shard_map/psum | solution.py:47
  132.1 7.9 fusion
  140.1 74.6 %psum.143 = bf16[1536,16]{0,1:T(8,128)(2,1)S(1)} all-reduce(bf16[1536,16]{0,1:T(8,128)(2,1)S(1)} %fusion), channel_id=1, replica_groups=mesh['dp'=8,'feat'=16] {'feat'}, use_global_device_ids=true, to_apply=%region_8.0 | all-reduce | flops 24576 | bytes 98304 | tf_op jit(solution)/shard_map/psum | solution.py:55
  214.8 7.0 convolution_convert_fusion.3
  221.8 53.6 %all-reduce.9.cloned.1.call-done = bf16[16,4096]{1,0:T(8,128)(2,1)} async-done(((bf16[16,4096]{1,0:T(8,128)(2,1)}), bf16[16,4096]{1,0:T(8,128)(2,1)}) %all-reduce.9.cloned.1.call-update) | async-done | bytes 131088 | tf_op jit(solution)/shard_map/psum | solution.py:61
  277.0 41.3 %all-reduce = (f32[]{:T(128)}, f32[]{:T(128)}) all-reduce(f32[]{:T(128)} %get-tuple-element.3, f32[]{:T(128)} %get-tuple-element.2), channel_id=1, replica_groups=mesh['dp'=8,'feat'=16] {'feat'}, use_global_device_ids=true, to_apply=%region_7.0 | all-reduce | flops 2 | bytes 16 | tf_op jit(solution)/shard_map/psum | solution.py:44
  321.2 36.3 %psum.146 = f32[]{:T(128)} all-reduce(f32[]{:T(128)} %multiply_reduce_fusion.5), channel_id=1, replica_groups=mesh['dp'=8,'feat'=16] {'feat'}, use_global_device_ids=true, to_apply=%region_14.0 | all-reduce | flops 1 | bytes 8 | tf_op jit(solution)/shard_map/psum | solution.py:44
  358.8 8.0 fusion.1
  366.8 71.7 %psum.147 = bf16[1536,16]{0,1:T(8,128)(2,1)S(1)} all-reduce(bf16[1536,16]{0,1:T(8,128)(2,1)S(1)} %fusion.1), channel_id=1, replica_groups=mesh['dp'=8,'feat'=16] {'feat'}, use_global_device_ids=true, to_apply=%region_15.0 | all-reduce | flops 24576 | bytes 98304 | tf_op jit(solution)/shard_map/psum | solution.py:55
  438.5 7.0 convolution_convert_fusion.2
  445.6 53.6 %all-reduce.11.cloned.1.call-done = bf16[16,4096]{1,0:T(8,128)(2,1)} async-done(((bf16[16,4096]{1,0:T(8,128)(2,1)}), bf16[16,4096]{1,0:T(8,128)(2,1)}) %all-reduce.11.cloned.1.call-update) | async-done | bytes 131088 | tf_op jit(solution)/shard_map/psum | solution.py:61
  500.9 41.3 %psum.149 = f32[]{:T(128)} all-reduce(f32[]{:T(128)} %multiply_reduce_fusion.4), channel_id=1, replica_groups=mesh['dp'=8,'feat'=16] {'feat'}, use_global_device_ids=true, to_apply=%region_19.0 | all-reduce | flops 1 | bytes 8 | tf_op jit(solution)/shard_map/psum | solution.py:44
  545.9 36.0 %psum.150 = f32[]{:T(128)} all-reduce(f32[]{:T(128)} %multiply_reduce_fusion.3), channel_id=1, replica_groups=mesh['dp'=8,'feat'=16] {'feat'}, use_global_device_ids=true, to_apply=%region_21.0 | all-reduce | flops 1 | bytes 8 | tf_op jit(solution)/shard_map/psum | solution.py:44
  582.5 8.0 fusion.2
  590.5 71.7 %psum.151 = bf16[1536,16]{0,1:T(8,128)(2,1)S(1)} all-reduce(bf16[1536,16]{0,1:T(8,128)(2,1)S(1)} %fusion.2), channel_id=1, replica_groups=mesh['dp'=8,'feat'=16] {'feat'}, use_global_device_ids=true, to_apply=%region_22.0 | all-reduce | flops 24576 | bytes 98304 | tf_op jit(solution)/shard_map/psum | solution.py:55
  662.2 7.0 convolution_convert_fusion.1
  669.3 53.6 %all-reduce.13.cloned.1.call-done = bf16[16,4096]{1,0:T(8,128)(2,1)} async-done(((bf16[16,4096]{1,0:T(8,128)(2,1)}), bf16[16,4096]{1,0:T(8,128)(2,1)}) %all-reduce.13.cloned.1.call-update) | async-done | bytes 131088 | tf_op jit(solution)/shard_map/psum | solution.py:61
  724.6 41.2 %psum.153 = f32[]{:T(128)} all-reduce(f32[]{:T(128)} %multiply_reduce_fusion.2), channel_id=1, replica_groups=mesh['dp'=8,'feat'=16] {'feat'}, use_global_device_ids=true, to_apply=%region_26.0 | all-reduce | flops 1 | bytes 8 | tf_op jit(solution)/shard_map/psum | solution.py:44
  769.4 36.2 %psum.154 = f32[]{:T(128)} all-reduce(f32[]{:T(128)} %multiply_reduce_fusion.1), channel_id=1, replica_groups=mesh['dp'=8,'feat'=16] {'feat'}, use_global_device_ids=true, to_apply=%region_28.0 | all-reduce | flops 1 | bytes 8 | tf_op jit(solution)/shard_map/psum | solution.py:44
  806.2 8.0 fusion.3
  814.2 71.7 %psum.155 = bf16[1536,16]{0,1:T(8,128)(2,1)S(1)} all-reduce(bf16[1536,16]{0,1:T(8,128)(2,1)S(1)} %fusion.3), channel_id=1, replica_groups=mesh['dp'=8,'feat'=16] {'feat'}, use_global_device_ids=true, to_apply=%region_29.0 | all-reduce | flops 24576 | bytes 98304 | tf_op jit(solution)/shard_map/psum | solution.py:55
  885.9 7.0 convolution_convert_fusion
  893.6 13.1 %psum.159 = f32[]{:T(128)} all-reduce(f32[]{:T(128)} %multiply_reduce_fusion.8), channel_id=1, replica_groups=mesh['dp'=8,'feat'=16] {'dp'}, use_global_device_ids=true, to_apply=%region_37.0 | all-reduce | flops 1 | bytes 8 | tf_op jit(solution)/shard_map/psum | solution.py:35
  906.7 39.8 %all-reduce.15.cloned.1.call-done = bf16[16,4096]{1,0:T(8,128)(2,1)} async-done(((bf16[16,4096]{1,0:T(8,128)(2,1)}), bf16[16,4096]{1,0:T(8,128)(2,1)}) %all-reduce.15.cloned.1.call-update) | async-done | bytes 131088 | tf_op jit(solution)/shard_map/psum | solution.py:61
  949.7 41.2 %psum.157 = f32[]{:T(128)} all-reduce(f32[]{:T(128)} %multiply_reduce_fusion), channel_id=1, replica_groups=mesh['dp'=8,'feat'=16] {'feat'}, use_global_device_ids=true, to_apply=%region_33.0 | all-reduce | flops 1 | bytes 8 | tf_op jit(solution)/shard_map/psum | solution.py:44
  992.3 7.9 fusion.4
  1000.2 69.6 %psum.158 = bf16[1536,16]{0,1:T(8,128)(2,1)S(1)} all-reduce(bf16[1536,16]{0,1:T(8,128)(2,1)S(1)} %fusion.4), channel_id=1, replica_groups=mesh['dp'=8,'feat'=16] {'feat'}, use_global_device_ids=true, to_apply=%region_34.0 | all-reduce | flops 24576 | bytes 98304 | tf_op jit(solution)/shard_map/psum | solution.py:73
  (43 shorter events, 16.1 us)
Async XLA Ops:
  7.2 8.7 copy-start.4
  7.2 57.8 %copy-start.5 = (s32[1536]{0:T(1024)S(1)}, s32[1536]{0:T(1024)}, u32[]{:S(2)}) copy-start(s32[1536]{0:T(1024)} %param.6) | copy-start | bytes 18436
  7.2 55.1 %all-gather.3.cloned.1.call-start = ((), (), s32[]{:S(2)}) async-start(), calls=%async_computation.5 | async-start | bytes 1671168 | tf_op jit(solution)/shard_map/all_gather | solution.py:26
  15.8 115.4 %copy-start.3 = (f32[16,4096]{1,0:T(8,128)S(1)}, f32[16,4096]{1,0:T(8,128)}, u32[]{:S(2)}) copy-start(f32[16,4096]{1,0:T(8,128)} %param.5) | copy-start | bytes 786436
  15.8 115.4 %all-reduce.7.cloned.1.call-start = ((), (), s32[]{:S(2)}) async-start(), calls=%async_computation | async-start | bytes 262144 | tf_op jit(solution)/shard_map/psum | solution.py:47
  72.0 203.5 %all-reduce.9.cloned.1.call-start = ((), (), s32[]{:S(2)}) async-start(), calls=%async_computation.1 | async-start | bytes 262144 | tf_op jit(solution)/shard_map/psum | solution.py:61
  221.8 277.4 %all-reduce.11.cloned.1.call-start = ((), (), s32[]{:S(2)}) async-start(), calls=%async_computation.2 | async-start | bytes 262144 | tf_op jit(solution)/shard_map/psum | solution.py:61
  366.8 132.3 %copy-start = (bf16[16,4096]{1,0:T(8,128)(2,1)S(1)}, bf16[16,4096]{1,0:T(8,128)(2,1)}, u32[]{:S(2)}) copy-start(bf16[16,4096]{1,0:T(8,128)(2,1)} %all-reduce.9.cloned.1.call-done) | copy-start | bytes 393220
  445.5 277.4 %all-reduce.13.cloned.1.call-start = ((), (), s32[]{:S(2)}) async-start(), calls=%async_computation.3 | async-start | bytes 262144 | tf_op jit(solution)/shard_map/psum | solution.py:61
  590.5 132.4 %copy-start.1 = (bf16[16,4096]{1,0:T(8,128)(2,1)S(1)}, bf16[16,4096]{1,0:T(8,128)(2,1)}, u32[]{:S(2)}) copy-start(bf16[16,4096]{1,0:T(8,128)(2,1)} %all-reduce.11.cloned.1.call-done) | copy-start | bytes 393220
  669.2 277.3 %all-reduce.15.cloned.1.call-start = ((), (), s32[]{:S(2)}) async-start(), calls=%async_computation.4 | async-start | bytes 262144 | tf_op jit(solution)/shard_map/psum | solution.py:61
  814.2 132.3 %copy-start.2 = (bf16[16,4096]{1,0:T(8,128)(2,1)S(1)}, bf16[16,4096]{1,0:T(8,128)(2,1)}, u32[]{:S(2)}) copy-start(bf16[16,4096]{1,0:T(8,128)(2,1)} %all-reduce.13.cloned.1.call-done) | copy-start | bytes 393220
Sparse Core Ops, SparseCore 0:
  16.0 46.3 all-gather.2
  72.1 59.0 all-reduce.6
  221.9 53.4 all-reduce.8
  445.7 53.4 all-reduce.10
  669.4 53.4 all-reduce.12
  893.1 53.4 all-reduce.14
